TPU v7x, 1024 devices: a whole 4x8x16 slice. The times are simulated.
1024 devices in a mesh: blk: 16 (over x, z_hi), grp: 64 (over z_lo, y, core).
Axes of the slice: x: 4, y: 8, z: 16 (z_hi: 4, z_lo: 4; z = z_hi * 4 + z_lo), core: 2. Of those that a mesh axis runs over, the one named last changes fastest.
Arguments:
- amplitudes: bfloat16 [8192, 49152], P(('blk', 'grp')), may hold values from -6 to 6
- integrals: bfloat16 [49152, 2048], P('grp', 'blk'), may hold values from -0.0390625 to 0.0390625
- tile_mask: int32 [1024, 384], P(('blk', 'grp')), may hold values from 0 to 1, as said below
- tile_size: int32 [384], replicated, may hold values from 64 to 128, as said below
Outputs:
- ladder: bfloat16 [8192, 2048], P(('blk', 'grp'))
Inputs may be any that keep to these rules, and one draw needn't show every extreme that they name: `tile_mask`: mask entries are 0 or 1; domains differ in how many of their tiles are live. `tile_size`: one tile is full and one is half full.
All inputs are finite; a program needn't handle non-finite values.
Results may differ from a plain program's by a relative error of at most 0.001.
Values may be sent and summed in bfloat16 or wider, within the bound.
A program may use at most 32 MiB of HBM per device.

v0:
```python
import jax
import jax.numpy as jnp
from jax import lax
from jax.sharding import PartitionSpec as P


def body(amplitudes, integrals, tile_mask, tile_size):
    row_count, width = amplitudes.shape
    tile_count = tile_size.shape[0]
    tile_width = width // tile_count
    lane_index = lax.broadcasted_iota(jnp.int32, (tile_count, tile_width), 1)
    live_tiles = (tile_mask[0][:, None] == 1) & (lane_index < tile_size[:, None])
    shaped = amplitudes.reshape(row_count, tile_count, tile_width)
    masked = jnp.where(live_tiles[None], shaped, jnp.zeros_like(shaped)).reshape(row_count, width)
    regrouped = lax.all_to_all(masked, "grp", split_axis=1, concat_axis=0, tiled=True)
    partial_value = jnp.dot(
        regrouped,
        lax.all_gather(integrals, "blk", axis=1, tiled=True),
        preferred_element_type=jnp.float32,
    )
    ladder = lax.psum_scatter(partial_value, "grp", scatter_dimension=0, tiled=True)
    return ladder.astype(jnp.bfloat16)


def solution(mesh):
    return jax.shard_map(
        body,
        mesh=mesh,
        in_specs=(P(("blk", "grp"), None), P("grp", "blk"), P(("blk", "grp"), None), P()),
        out_specs=P(("blk", "grp"), None),
        check_vma=False,
    )
```

profile of v0, /device:TPU:1, one launch (start us, length us, event | category | flops | bytes accessed | tf_op | source)
XLA Modules:
  0.0 452.1 jit_solution(17698749344518637466)
XLA Ops:
  6.5 0.0 all-gather.2.cloned.1.call-start
  6.5 0.7 all-gather.2.cloned.1.call-update
  7.3 0.0 reduce-scatter.2.cloned.1.call-start
  7.3 0.7 compare_reduce_fusion
  8.0 1.7 lt.14
  9.7 0.1 fusion.2
  9.8 1.3 broadcast_select_fusion
  11.1 44.1 %all_to_all.19 = bf16[8,64,768]{2,0,1:T(8,128)(2,1)S(1)} all-to-all(bf16[8,64,768]{2,0,1:T(8,128)(2,1)S(1)} %bitcast.14), channel_id=1, replica_groups=mesh['blk'=16,'grp'=64] {'grp'}, dimensions={1} | all-to-all | bytes 1572864 | tf_op jit(solution)/shard_map/all_to_all | solution.py:15
  55.2 90.9 %all-gather.2.cloned.1.call-done = bf16[768,2048]{1,0:T(8,128)(2,1)} async-done(((bf16[768,128]{1,0:T(8,128)(2,1)}), bf16[768,2048]{1,0:T(8,128)(2,1)}) %all-gather.2.cloned.1.call-update) | async-done | bytes 3145744 | tf_op jit(solution)/shard_map/all_gather | solution.py:18
  146.1 5.6 %fusion = f32[512,2048]{1,0:T(8,128)} fusion(bf16[768,2048]{1,0:T(8,128)(2,1)} %all-gather.2.cloned.1.call-done, bf16[8,64,768]{2,0,1:T(8,128)(2,1)S(1)} %all_to_all.19), kind=kOutput, calls=%fused_computation | convolution fusion | flops 1610612736 | bytes 8126464 | tf_op jit(solution)/shard_map/dot_general | solution.py:16
  151.7 0.0 reduce-scatter.2.cloned.1.call-update
  151.7 292.0 %reduce-scatter.2.cloned.1.call-done = f32[8,2048]{1,0:T(8,128)} async-done(((f32[512,2048]{1,0:T(8,128)}), f32[8,2048]{1,0:T(8,128)}) %reduce-scatter.2.cloned.1.call-update) | async-done | bytes 65552 | tf_op jit(solution)/shard_map/reduce_scatter | solution.py:21
  443.8 1.5 convert_element_type.3
Async XLA Ops:
  6.5 139.6 %all-gather.2.cloned.1.call-start = ((), (), s32[]{:S(2)}) async-start(), calls=%async_computation.2 | async-start | bytes 3342336 | tf_op jit(solution)/shard_map/all_gather | solution.py:18
  7.3 436.5 %reduce-scatter.2.cloned.1.call-start = ((), (), s32[]{:S(2)}) async-start(), calls=%async_computation.3 | async-start | bytes 4259840 | tf_op jit(solution)/shard_map/reduce_scatter | solution.py:21
Sparse Core Ops, SparseCore 0:
  11.5 134.5 all-gather.1
  151.9 291.8 reduce-scatter.1
where the time goes:
time: 456 us; the launch traced here: 452 us
  waiting for transfers between devices  384 us (84%)
  blocking collectives  44.1 us (10%)
  between operations  13.4 us (3%)
  matrix products  5.62 us (1%)
    reduce_scatter x1, waiting for transfers between devices, body(): lax.psum_scatter(partial_value, 'grp', scatter_dimension=0, tiled=True)  292 us
    all_gather x1, waiting for transfers between devices, body(): lax.all_gather(integrals, 'blk', axis=1, tiled=True)  90.9 us
    all_to_all x1, blocking collectives, body(): lax.all_to_all(masked, 'grp', split_axis=1, concat_axis=0, tiled=True)  44.1 us
  transfers between devices with their start and end apart: 2, of which 2 were waited for; matrix products, arithmetic and copies ran while one was open for 1% of the time, Pallas kernels for 0%

commit v1 on v0

v1 whole, which is shorter than its diff:
```python
import jax
import jax.numpy as jnp
from jax import lax
from jax.experimental import pallas as pl
from jax.experimental.pallas import tpu as pltpu
from jax.sharding import Mesh, PartitionSpec as P

NX, NZH, NZL, NY, NC = 4, 4, 4, 8, 2
NZ = NZH * NZL
NCHIP = NX * NY
NSTEP = 32
MESH = pl.DeviceIdType.MESH


def kernel(mask_ref, size_ref, amp_ref, int_ref, out_ref,
           am, a2, bb, cb, rxp, rxm, ryp, rym, sb, so,
           a_send, a_recv, a_loc, sib_send, sib_recv, b_send, b_recv,
           z_send, z_recv, x_send, x_recv, y_send, y_recv, o_send, o_recv):
    x = lax.axis_index("x")
    zh = lax.axis_index("zh")
    zl = lax.axis_index("zl")
    y = lax.axis_index("y")
    c = lax.axis_index("c")
    z = zh * NZL + zl
    me = x * NY + y
    other = 1 - c

    barrier = pltpu.get_barrier_semaphore()

    def greet(i, _):
        xx = lax.rem(x + i // NY, NX)
        yy = lax.rem(y + lax.rem(i, NY), NY)
        pl.semaphore_signal(barrier, inc=1, device_id={"x": xx, "y": yy}, device_id_type=MESH)
        return 0

    lax.fori_loop(1, NCHIP, greet, 0)
    for dx in range(NX):
        pl.semaphore_signal(barrier, inc=1, device_id={"x": lax.rem(x + dx, NX), "c": other}, device_id_type=MESH)
    zup = lax.rem(z + 1, NZ)
    zdn = lax.rem(z + NZ - 1, NZ)
    up = {"zh": zup // NZL, "zl": lax.rem(zup, NZL)}
    dn = {"zh": zdn // NZL, "zl": lax.rem(zdn, NZL)}
    pl.semaphore_signal(barrier, inc=1, device_id=up, device_id_type=MESH)
    pl.semaphore_signal(barrier, inc=1, device_id=dn, device_id_type=MESH)

    lane = lax.broadcasted_iota(jnp.int32, (8, 128), 1)

    def live(q, _):
        for t in range(12):
            tile = q * 12 + t
            limit = jnp.where(mask_ref[0, tile] == 1, size_ref[tile], 0)
            col = pl.multiple_of(tile * 128, 128)
            v = amp_ref[:, pl.ds(col, 128)].astype(jnp.float32)
            am[q, :, t * 128:(t + 1) * 128] = jnp.where(lane < limit, v, 0.0).astype(jnp.bfloat16)
        return 0

    lax.fori_loop(0, NCHIP, live, 0)
    pl.semaphore_wait(barrier, NCHIP - 1 + NX + 2)

    jb = lax.rem(x, 2)
    cdst = x // 2
    stay = (x == zl) & (c == cdst)

    def b_src(h):
        return int_ref.at[h * 192:(h + 1) * 192, :]

    @pl.when(stay)
    def _():
        for h in range(4):
            pltpu.make_async_copy(b_src(h), bb.at[jb, zh, c * 4 + h], b_recv.at[jb, c * 4 + h]).start()

    def b_copy(h):
        return pltpu.make_async_remote_copy(
            src_ref=b_src(h), dst_ref=bb.at[jb, zh, c * 4 + h],
            send_sem=b_send.at[h], recv_sem=b_recv.at[jb, c * 4 + h],
            device_id={"x": zl, "c": cdst}, device_id_type=MESH)

    @pl.when(jnp.logical_not(stay))
    def _():
        for h in range(4):
            b_copy(h).start()

    def a_copy(i):
        xx = lax.rem(x + i // NY, NX)
        yy = lax.rem(y + lax.rem(i, NY), NY)
        return pltpu.make_async_remote_copy(
            src_ref=am.at[xx * NY + yy], dst_ref=a2.at[c, pl.ds(pl.multiple_of(me * 8, 8), 8), :],
            send_sem=a_send.at[i], recv_sem=a_recv.at[i],
            device_id={"x": xx, "y": yy}, device_id_type=MESH)

    def a_start(i, _):
        a_copy(i).start()
        return 0

    lax.fori_loop(1, NCHIP, a_start, 0)
    a_own = pltpu.make_async_copy(am.at[me], a2.at[c, pl.ds(pl.multiple_of(me * 8, 8), 8), :], a_loc)
    a_own.start()

    sib_copy = pltpu.make_async_remote_copy(
        src_ref=a2.at[c], dst_ref=a2.at[c], send_sem=sib_send, recv_sem=sib_recv,
        device_id={"c": other}, device_id_type=MESH)

    def a_finish():
        def a_wait(i, _):
            a_copy(i).wait_recv()
            return 0
        lax.fori_loop(1, NCHIP, a_wait, 0)
        a_own.wait()
        sib_copy.start()

    p = lax.rem(z - x + NZ, NZL)
    sp = lax.rem((z - x + NZ) // NZL, NZH)
    dm = lax.rem(NZL - p, NZL)

    def z_parts(n, way):
        j = n // 16
        k = lax.rem(n, 16) // 8
        ch = lax.rem(n, 8)
        if way == 0:
            s = lax.rem(sp - k + NZH, NZH)
            sends = jnp.logical_not((p == 3) & (k == 1) & (ch >= 4))
        else:
            s = lax.rem(sp + jnp.where(p == 0, 0, 1) + k, NZH)
            sends = jnp.logical_not((p == 1) & (k == 1) & (ch < 4))
        copy = pltpu.make_async_remote_copy(
            src_ref=bb.at[j, s, ch], dst_ref=bb.at[j, s, ch],
            send_sem=z_send.at[way, n], recv_sem=z_recv.at[way, j, s, ch],
            device_id=up if way == 0 else dn, device_id_type=MESH)
        return j, k, s, ch, sends, copy

    def z_step(n, way):
        @pl.when((n >= 0) & (n < NSTEP))
        def _():
            j, k, s, ch, sends, copy = z_parts(n, way)
            own = (p == 0) & (k == 0)

            @pl.when(jnp.logical_not(own))
            def _():
                copy.wait_recv()

            if way == 0:
                @pl.when(own)
                def _():
                    pltpu.make_async_copy(bb.at[j, s, ch], bb.at[j, s, ch], b_recv.at[j, ch]).wait()

            @pl.when(sends)
            def _():
                copy.start()

    def z_slots(lo, hi):
        def slot(t, _):
            z_step(t - p, 0)
            z_step(t - dm, 1)
            return 0
        lax.fori_loop(lo, hi, slot, 0)

    def z_far(j):
        @pl.when(p == 0)
        def _():
            s = lax.rem(sp + 2, NZH)
            for ch in range(8):
                way = 0 if ch < 4 else 1
                pltpu.make_async_copy(bb.at[j, s, ch], bb.at[j, s, ch], z_recv.at[way, j, s, ch]).wait()

    def product(j):
        for h in range(2):
            rhs = jnp.concatenate([bb[j, 2 * h].reshape(1536, 128), bb[j, 2 * h + 1].reshape(1536, 128)], axis=1)
            for cc in range(2):
                part = jnp.dot(a2[cc], rhs, preferred_element_type=jnp.float32)
                cb[j, :, :, cc, :, h * 256:(h + 1) * 256] = part.reshape(NX, NY, 8, 256)

    xs = [lax.rem(x + d, NX) for d in range(NX)]
    ys = [lax.rem(y + d, NY) for d in range(NY)]
    right, left = {"x": xs[1]}, {"x": xs[3]}
    above, below = {"y": ys[1]}, {"y": ys[7]}

    def x_copy(j, way, m):
        if way == 0:
            src = (cb.at[j, xs[2], 0:4], cb.at[j, xs[1], 4:8], cb.at[j, xs[1], 0:4])[m]
        else:
            src = (cb.at[j, xs[2], 4:8], cb.at[j, xs[3], 0:4], cb.at[j, xs[3], 4:8])[m]
        return pltpu.make_async_remote_copy(
            src_ref=src, dst_ref=(rxp, rxm)[way].at[j, m],
            send_sem=x_send.at[j, way, m], recv_sem=x_recv.at[j, way, m],
            device_id=(right, left)[way], device_id_type=MESH)

    def y_copy(j, way, m):
        row = ys[4 - m] if way == 0 else ys[4 + m]
        if m == 0:
            src = cb.at[j, x, row, way]
            dst = (ryp, rym)[way].at[j, 0, way]
        else:
            src = cb.at[j, x, row]
            dst = (ryp, rym)[way].at[j, m]
        return pltpu.make_async_remote_copy(
            src_ref=src, dst_ref=dst,
            send_sem=y_send.at[j, way, m], recv_sem=y_recv.at[j, way, m],
            device_id=(above, below)[way], device_id_type=MESH)

    def o_copy(j):
        return pltpu.make_async_remote_copy(
            src_ref=sb.at[j], dst_ref=so.at[j], send_sem=o_send.at[j], recv_sem=o_recv.at[j],
            device_id={"c": other}, device_id_type=MESH)

    def x_first(j):
        for m in range(2):
            x_copy(j, 0, m).start()
            x_copy(j, 1, m).start()

    def x_second(j):
        x_copy(j, 0, 0).wait_recv()
        cb[j, xs[1], 0:4] = cb[j, xs[1], 0:4] + rxp[j, 0]
        x_copy(j, 0, 2).start()
        x_copy(j, 1, 0).wait_recv()
        cb[j, xs[3], 4:8] = cb[j, xs[3], 4:8] + rxm[j, 0]
        x_copy(j, 1, 2).start()

    def x_last(j):
        for m in range(1, 3):
            x_copy(j, 0, m).wait_recv()
            x_copy(j, 1, m).wait_recv()
        cb[j, x, 0:4] = cb[j, x, 0:4] + rxp[j, 2] + rxm[j, 1]
        cb[j, x, 4:8] = cb[j, x, 4:8] + rxp[j, 1] + rxm[j, 2]
        y_copy(j, 0, 0).start()
        y_copy(j, 1, 0).start()

    def y_next(j, m):
        for way in range(2):
            row = ys[4 - m] if way == 0 else ys[4 + m]
            buf = (ryp, rym)[way]
            y_copy(j, way, m - 1).wait_recv()
            if m == 1:
                cb[j, x, row, way] = cb[j, x, row, way] + buf[j, 0, way]
            else:
                cb[j, x, row] = cb[j, x, row] + buf[j, m - 1]
            y_copy(j, way, m).start()

    def y_last(j):
        y_copy(j, 0, 3).wait_recv()
        y_copy(j, 1, 3).wait_recv()
        sb[j] = (cb[j, x, y, other] + ryp[j, 3, other] + rym[j, 3, other]).astype(jnp.bfloat16)
        o_copy(j).start()
        mine = (cb[j, x, y, c] + ryp[j, 3, c] + rym[j, 3, c]).astype(jnp.bfloat16)
        out_ref[:, pl.ds(pl.multiple_of((2 * c + j) * 512, 512), 512)] = mine

    def tail(j):
        return [lambda: x_second(j), lambda: x_last(j)] + [
            (lambda m=m: y_next(j, m)) for m in range(1, 4)] + [lambda: y_last(j)]

    z_slots(0, 14)
    a_finish()
    z_slots(14, 19)
    z_far(0)
    sib_copy.wait_recv()
    product(0)
    x_first(0)
    at = 19
    for step, event in zip((5, 3, 2, 2, 2, 2), tail(0)):
        z_slots(at, at + step)
        at += step
        event()
    z_slots(at, NSTEP + 3)
    z_far(1)
    product(1)
    x_first(1)
    for event in tail(1):
        event()

    for j in range(2):
        o_copy(j).wait_recv()
        out_ref[:, pl.ds(pl.multiple_of((2 * other + j) * 512, 512), 512)] = so[j]

    def a_left(i, _):
        a_copy(i).wait_send()
        return 0

    lax.fori_loop(1, NCHIP, a_left, 0)
    sib_copy.wait_send()

    @pl.when(jnp.logical_not(stay))
    def _():
        for h in range(4):
            b_copy(h).wait_send()

    def z_left(n, _):
        for way in range(2):
            parts = z_parts(n, way)

            @pl.when(parts[4])
            def _():
                parts[5].wait_send()
        return 0

    lax.fori_loop(0, NSTEP, z_left, 0)
    for j in range(2):
        for way in range(2):
            for m in range(3):
                x_copy(j, way, m).wait_send()
            for m in range(4):
                y_copy(j, way, m).wait_send()
        o_copy(j).wait_send()


def body(amplitudes, integrals, tile_mask, tile_size):
    dma = pltpu.SemaphoreType.DMA
    f32, bf16 = jnp.float32, jnp.bfloat16
    return pl.pallas_call(
        kernel,
        out_shape=jax.ShapeDtypeStruct((8, 2048), bf16),
        in_specs=[pl.BlockSpec(memory_space=pltpu.SMEM)] * 2 + [pl.BlockSpec(memory_space=pltpu.VMEM)] * 2,
        out_specs=pl.BlockSpec(memory_space=pltpu.VMEM),
        scratch_shapes=[
            pltpu.VMEM((NCHIP, 8, 1536), bf16),
            pltpu.VMEM((2, 256, 1536), bf16),
            pltpu.VMEM((2, NZH, 8, 192, 128), bf16),
            pltpu.VMEM((2, NX, NY, 2, 8, 512), f32),
            pltpu.VMEM((2, 3, 4, 2, 8, 512), f32),
            pltpu.VMEM((2, 3, 4, 2, 8, 512), f32),
            pltpu.VMEM((2, 4, 2, 8, 512), f32),
            pltpu.VMEM((2, 4, 2, 8, 512), f32),
            pltpu.VMEM((2, 8, 512), bf16),
            pltpu.VMEM((2, 8, 512), bf16),
            dma((NCHIP,)), dma((NCHIP,)), dma(()), dma(()), dma(()),
            dma((4,)), dma((2, 8)),
            dma((2, NSTEP)), dma((2, 2, NZH, 8)),
            dma((2, 2, 3)), dma((2, 2, 3)),
            dma((2, 2, 4)), dma((2, 2, 4)),
            dma((2,)), dma((2,)),
        ],
        compiler_params=pltpu.CompilerParams(collective_id=0, has_side_effects=True),
    )(tile_mask, tile_size, amplitudes, integrals)


def solution(mesh):
    axes = ("x", "zh", "zl", "y", "c")
    fine = Mesh(mesh.devices.reshape(NX, NZH, NZL, NY, NC), axes)
    return jax.shard_map(
        body,
        mesh=fine,
        in_specs=(P(axes, None), P(("zl", "y", "c"), ("x", "zh")), P(axes, None), P()),
        out_specs=P(axes, None),
        check_vma=False,
    )
```

time: 456 us -> 158 us (0.35)
  waiting for transfers between devices: 384 us -> 0 us
  Pallas kernels: 0 us -> 156 us
  blocking collectives: 44.1 us -> 0 us
  between operations: 13.4 us -> 0.01 us
  matrix products: 5.62 us -> 0 us
    reduce_scatter x1 -> x0, waiting for transfers between devices: 292 us -> none  [body(): lax.psum_scatter(partial_value, 'grp', scatter_dimension=0, tiled=True)]
    pallas_call x0 -> x1, Pallas kernels: none -> 156 us  [body(): pl.pallas_call(kernel, out_shape=jax.ShapeDtypeStruct((8, 2048), bf16), i...]
    all_gather x1 -> x0, waiting for transfers between devices: 90.9 us -> none  [body(): lax.all_gather(integrals, 'blk', axis=1, tiled=True)]
    all_to_all x1 -> x0, blocking collectives: 44.1 us -> none  [body(): lax.all_to_all(masked, 'grp', split_axis=1, concat_axis=0, tiled=True)]
    dot_general x1 -> x0, matrix products: 5.62 us -> none  [body(): jnp.dot(regrouped, lax.all_gather(integrals, 'blk', axis=1, tiled=True),...]
  transfers between devices with their start and end apart: 2 -> 0, of which waited for: 2 -> 0; matrix products, arithmetic and copies ran while one was open for 1% -> 0% of each run, Pallas kernels for 0% -> 0%
where the time goes in v1:
time: 158 us
  Pallas kernels  156 us (99%)
    pallas_call x1, Pallas kernels, body(): pl.pallas_call(kernel, out_shape=jax.ShapeDtypeStruct((8, 2048), bf16), i...  156 us

profile of v1, /device:TPU:1, one launch (start us, length us, event | category | flops | bytes accessed | tf_op | source)
XLA Modules:
  0.0 157.7 jit_solution(12914268641407905049)
XLA Ops:
  0.0 156.3 %shard_map.46 = bf16[8,2048]{1,0:T(8,128)(2,1)} custom-call(s32[1,384]{1,0:T(1,128)} %mask_ref.1, s32[384]{0:T(512)} %size_ref.1, bf16[8,49152]{1,0:T(8,128)(2,1)} %amp_ref.1, bf16[768,128]{1,0:T(8,128)(2,1)} %int_ref.1), custom_call_target="tpu_custom_call" | custom-call | tf_op jit(solution)/shard_map/pallas_call | solution.py:307
  156.3 1.4 copy.6

commit v2 on v1

v2 whole, which is shorter than its diff:
```python
import jax
import jax.numpy as jnp
from jax import lax
from jax.experimental import pallas as pl
from jax.experimental.pallas import tpu as pltpu
from jax.sharding import Mesh, PartitionSpec as P

NX, NZH, NZL, NY, NC = 4, 4, 4, 8, 2
NZ = NZH * NZL
NCHIP = NX * NY
NPIECE = 4
FAR = NZ // 2
NSTEP = NPIECE * FAR
ROUNDS = NZH
MESH = pl.DeviceIdType.MESH


def kernel(mask_ref, size_ref, amp_ref, int_ref, out_ref,
           am, a2, bb, ca, cb, rxp, rxm, ryp, rym, fa, fb, sb, so,
           a_send, a_recv, a_loc, sib_send, sib_recv, b_send, b_recv,
           z_send, z_recv, x_send, x_recv, y_send, y_recv, fa_send, fa_recv, fb_send, fb_recv, o_send, o_recv):
    x = lax.axis_index("x")
    zh = lax.axis_index("zh")
    zl = lax.axis_index("zl")
    y = lax.axis_index("y")
    c = lax.axis_index("c")
    z = zh * NZL + zl
    me = x * NY + y
    other = 1 - c

    barrier = pltpu.get_barrier_semaphore()

    def greet(i, _):
        xx = lax.rem(x + i // NY, NX)
        yy = lax.rem(y + lax.rem(i, NY), NY)
        pl.semaphore_signal(barrier, inc=1, device_id={"x": xx, "y": yy}, device_id_type=MESH)
        return 0

    lax.fori_loop(1, NCHIP, greet, 0)
    for dx in range(NX):
        pl.semaphore_signal(barrier, inc=1, device_id={"x": lax.rem(x + dx, NX), "c": other}, device_id_type=MESH)
    zup = lax.rem(z + 1, NZ)
    zdn = lax.rem(z + NZ - 1, NZ)
    up = {"zh": zup // NZL, "zl": lax.rem(zup, NZL)}
    dn = {"zh": zdn // NZL, "zl": lax.rem(zdn, NZL)}
    pl.semaphore_signal(barrier, inc=1, device_id=up, device_id_type=MESH)
    pl.semaphore_signal(barrier, inc=1, device_id=dn, device_id_type=MESH)

    pl.semaphore_wait(barrier, NCHIP - 1 + NX + 2)

    jb = lax.rem(x, 2)
    cdst = x // 2

    def b_src(h, half):
        return int_ref.at[(2 * h + half) * 192:(2 * h + half + 1) * 192, :]

    def b_copy(h, half):
        return pltpu.make_async_remote_copy(
            src_ref=b_src(h, half), dst_ref=bb.at[jb, zh, zl, half],
            send_sem=b_send.at[h, half], recv_sem=b_recv.at[jb, half],
            device_id={"x": 2 * c + h, "c": cdst}, device_id_type=MESH)

    def b_stays(h):
        return x == 2 * c + h

    for half in range(2):
        for h in range(2):
            @pl.when(b_stays(h))
            def _():
                pltpu.make_async_copy(b_src(h, half), bb.at[jb, zh, zl, half], b_recv.at[jb, half]).start()

            @pl.when(jnp.logical_not(b_stays(h)))
            def _():
                b_copy(h, half).start()

    lane = lax.broadcasted_iota(jnp.int32, (8, 128), 1)

    def live(q, _):
        for t in range(12):
            tile = ((t // 3) * 2 * NY + 2 * lax.rem(q, NY)) * 6 + (q // NY) * 3 + t % 3
            limit = jnp.where(mask_ref[0, tile] == 1, size_ref[tile], 0)
            col = pl.multiple_of(tile * 128, 128)
            v = amp_ref[:, pl.ds(col, 128)].astype(jnp.float32)
            am[q, :, t * 128:(t + 1) * 128] = jnp.where(lane < limit, v, 0.0).astype(jnp.bfloat16)
        return 0

    lax.fori_loop(0, NCHIP, live, 0)
    def a_copy(i):
        xx = lax.rem(x + i // NY, NX)
        yy = lax.rem(y + lax.rem(i, NY), NY)
        return pltpu.make_async_remote_copy(
            src_ref=am.at[xx * NY + yy], dst_ref=a2.at[c, pl.ds(pl.multiple_of(me * 8, 8), 8), :],
            send_sem=a_send.at[i], recv_sem=a_recv.at[i],
            device_id={"x": xx, "y": yy}, device_id_type=MESH)

    def a_start(i, _):
        a_copy(i).start()
        return 0

    lax.fori_loop(1, NCHIP, a_start, 0)
    a_own = pltpu.make_async_copy(am.at[me], a2.at[c, pl.ds(pl.multiple_of(me * 8, 8), 8), :], a_loc)
    a_own.start()

    sib_copy = pltpu.make_async_remote_copy(
        src_ref=a2.at[c], dst_ref=a2.at[c], send_sem=sib_send, recv_sem=sib_recv,
        device_id={"c": other}, device_id_type=MESH)

    def a_finish():
        def a_wait(i, _):
            a_copy(i).wait_recv()
            return 0
        lax.fori_loop(1, NCHIP, a_wait, 0)
        a_own.wait()
        sib_copy.start()

    def z_parts(n, way):
        d = n // NPIECE
        i = lax.rem(n, NPIECE)
        zs = lax.rem(z + (NZ - d if way == 0 else d), NZ)
        ref = bb.at[lax.rem(i, 2), zs // NZL, lax.rem(zs, NZL), i // 2]
        return d, i, ref

    def z_copy(n, way):
        _, _, ref = z_parts(n, way)
        return pltpu.make_async_remote_copy(
            src_ref=ref, dst_ref=ref, send_sem=z_send.at[way, n], recv_sem=z_recv.at[way, n + NPIECE],
            device_id=up if way == 0 else dn, device_id_type=MESH)

    def z_arrive(n, way):
        _, _, ref = z_parts(n, way)
        pltpu.make_async_copy(ref, ref, z_recv.at[way, n]).wait()

    def z_passes(n, way):
        d, i, _ = z_parts(n, way)
        near = (i < NPIECE // 2) if way == 0 else (i >= NPIECE // 2)
        return (d < FAR - 1) | near

    def z_slots(lo, hi):
        def slot(n, _):
            @pl.when(n < NPIECE)
            def _():
                _, i, ref = z_parts(n, 0)
                pltpu.make_async_copy(ref, ref, b_recv.at[lax.rem(i, 2), i // 2]).wait()

            for way in range(2):
                @pl.when(n >= NPIECE)
                def _():
                    z_arrive(n, way)

                @pl.when(z_passes(n, way))
                def _():
                    z_copy(n, way).start()
            return 0
        lax.fori_loop(lo, hi, slot, 0)

    def z_far():
        for i in range(NPIECE):
            z_arrive(NSTEP + i, 0 if i < NPIECE // 2 else 1)

    side = jnp.where(zl < NZL // 2, NZH - 1, 1)
    block = [zh, lax.rem(zh + side, NZH), lax.rem(zh + NZH - side, NZH), lax.rem(zh + NZH // 2, NZH)]

    def product(r):
        rhs = jnp.concatenate([bb[0, block[r]].reshape(1536, 128), bb[1, block[r]].reshape(1536, 128)], axis=1)
        for cc in range(2):
            part = jnp.dot(a2[cc], rhs, preferred_element_type=jnp.float32).reshape(NX, NY, 8, 256)
            ca[r, :, :, cc] = part[:, :, :, :128]
            for xx in range(NX):
                cb[r, :, xx, cc] = part[xx, :, :, 128:]

    xs = [lax.rem(x + d, NX) for d in range(NX)]
    ys = [lax.rem(y + d, NY) for d in range(NY)]

    def x_copy(j, way, m):
        if way == 0:
            src = (ca.at[j, xs[2], 0:4], ca.at[j, xs[1], 4:8], ca.at[j, xs[1], 0:4])[m]
        else:
            src = (ca.at[j, xs[2], 4:8], ca.at[j, xs[3], 0:4], ca.at[j, xs[3], 4:8])[m]
        return pltpu.make_async_remote_copy(
            src_ref=src, dst_ref=(rxp, rxm)[way].at[j, m],
            send_sem=x_send.at[j, way, m], recv_sem=x_recv.at[j, way, m],
            device_id={"x": xs[1] if way == 0 else xs[3]}, device_id_type=MESH)

    def y_copy(j, way, m):
        row = ys[4 - m] if way == 0 else ys[4 + m]
        buf = (ryp, rym)[way]
        if m == 0:
            src = cb.at[j, row, 2 * way:2 * way + 2]
            dst = buf.at[j, 0, 2 * way:2 * way + 2]
        else:
            src = cb.at[j, row]
            dst = buf.at[j, m]
        return pltpu.make_async_remote_copy(
            src_ref=src, dst_ref=dst,
            send_sem=y_send.at[j, way, m], recv_sem=y_recv.at[j, way, m],
            device_id={"y": ys[1] if way == 0 else ys[7]}, device_id_type=MESH)

    def fa_copy(j, d):
        return pltpu.make_async_remote_copy(
            src_ref=ca.at[j, x, ys[d]], dst_ref=fa.at[j, d], send_sem=fa_send.at[j, d], recv_sem=fa_recv.at[j, d],
            device_id={"y": ys[d]}, device_id_type=MESH)

    def fb_copy(j, d):
        return pltpu.make_async_remote_copy(
            src_ref=cb.at[j, y, xs[d]], dst_ref=fb.at[j, d], send_sem=fb_send.at[j, d], recv_sem=fb_recv.at[j, d],
            device_id={"x": xs[d]}, device_id_type=MESH)

    def o_copy(j):
        return pltpu.make_async_remote_copy(
            src_ref=sb.at[j], dst_ref=so.at[j], send_sem=o_send.at[j], recv_sem=o_recv.at[j],
            device_id={"c": other}, device_id_type=MESH)

    def first(j):
        product(j)
        y_copy(j, 0, 0).start()
        y_copy(j, 1, 0).start()
        for m in range(2):
            x_copy(j, 0, m).start()
            x_copy(j, 1, m).start()

    def x_second(j):
        x_copy(j, 0, 0).wait_recv()
        ca[j, xs[1], 0:4] = ca[j, xs[1], 0:4] + rxp[j, 0]
        x_copy(j, 0, 2).start()
        x_copy(j, 1, 0).wait_recv()
        ca[j, xs[3], 4:8] = ca[j, xs[3], 4:8] + rxm[j, 0]
        x_copy(j, 1, 2).start()

    def x_last(j):
        for m in range(1, 3):
            x_copy(j, 0, m).wait_recv()
            x_copy(j, 1, m).wait_recv()
        ca[j, x, 0:4] = ca[j, x, 0:4] + rxp[j, 2] + rxm[j, 1]
        ca[j, x, 4:8] = ca[j, x, 4:8] + rxp[j, 1] + rxm[j, 2]
        for d in (4, 3, 5, 2, 6, 1, 7):
            fa_copy(j, d).start()

    def y_next(j, m):
        for way in range(2):
            row = ys[4 - m] if way == 0 else ys[4 + m]
            buf = (ryp, rym)[way]
            y_copy(j, way, m - 1).wait_recv()
            if m == 1:
                part = slice(2 * way, 2 * way + 2)
                cb[j, row, part] = cb[j, row, part] + buf[j, 0, part]
            else:
                cb[j, row] = cb[j, row] + buf[j, m - 1]
            y_copy(j, way, m).start()

    def y_last(j):
        y_copy(j, 0, 3).wait_recv()
        y_copy(j, 1, 3).wait_recv()
        cb[j, y] = cb[j, y] + ryp[j, 3] + rym[j, 3]
        for d in (2, 1, 3):
            fb_copy(j, d).start()

    def finish(j):
        for d in range(1, NY):
            fa_copy(j, d).wait_recv()
        for d in range(1, NX):
            fb_copy(j, d).wait_recv()

        def rows(core):
            left = ca[j, x, y, core]
            for d in range(1, NY):
                left = left + fa[j, d, core]
            right = cb[j, y, x, core]
            for d in range(1, NX):
                right = right + fb[j, d, core]
            return left.astype(jnp.bfloat16), right.astype(jnp.bfloat16)

        left, right = rows(other)
        sb[j, :, :128] = left
        sb[j, :, 128:] = right
        o_copy(j).start()
        store(j, c, *rows(c))

    def store(j, core, left, right):
        for half, value in enumerate((left, right)):
            col = ((2 * core + half) * NZH + block[j]) * 128
            out_ref[:, pl.ds(pl.multiple_of(col, 128), 128)] = value

    def e1(r):
        y_next(r, 1)
        x_second(r)

    def e3(r):
        x_last(r)
        y_next(r, 3)

    z_slots(0, 24)
    a_finish()
    z_slots(24, 27)
    sib_copy.wait_recv()
    first(0)
    z_slots(27, 29)
    first(1)
    e1(0)
    z_slots(29, 31)
    y_next(0, 2)
    e1(1)
    z_slots(31, 32)
    first(2)
    e3(0)
    z_far()
    first(3)
    y_next(1, 2)
    y_last(0)
    e1(2)
    e1(3)
    e3(1)
    y_next(2, 2)
    y_next(3, 2)
    y_last(1)
    finish(0)
    e3(2)
    e3(3)
    finish(1)
    y_last(2)
    y_last(3)
    finish(2)
    finish(3)

    for j in range(ROUNDS):
        o_copy(j).wait_recv()
        store(j, other, so[j, :, :128], so[j, :, 128:])

    def a_left(i, _):
        a_copy(i).wait_send()
        return 0

    lax.fori_loop(1, NCHIP, a_left, 0)
    sib_copy.wait_send()

    for h in range(2):
        @pl.when(jnp.logical_not(b_stays(h)))
        def _():
            for half in range(2):
                b_copy(h, half).wait_send()

    def z_left(n, _):
        for way in range(2):
            @pl.when(z_passes(n, way))
            def _():
                z_copy(n, way).wait_send()
        return 0

    lax.fori_loop(0, NSTEP, z_left, 0)
    for j in range(ROUNDS):
        for way in range(2):
            for m in range(3):
                x_copy(j, way, m).wait_send()
            for m in range(4):
                y_copy(j, way, m).wait_send()
        for d in range(1, NY):
            fa_copy(j, d).wait_send()
        for d in range(1, NX):
            fb_copy(j, d).wait_send()
        o_copy(j).wait_send()


def body(amplitudes, integrals, tile_mask, tile_size):
    dma = pltpu.SemaphoreType.DMA
    f32, bf16 = jnp.float32, jnp.bfloat16
    return pl.pallas_call(
        kernel,
        out_shape=jax.ShapeDtypeStruct((8, 2048), bf16),
        in_specs=[pl.BlockSpec(memory_space=pltpu.SMEM)] * 2 + [pl.BlockSpec(memory_space=pltpu.VMEM)] * 2,
        out_specs=pl.BlockSpec(memory_space=pltpu.VMEM),
        scratch_shapes=[
            pltpu.VMEM((NCHIP, 8, 1536), bf16),
            pltpu.VMEM((2, 256, 1536), bf16),
            pltpu.VMEM((2, NZH, NZL, 2, 192, 128), bf16),
            pltpu.VMEM((ROUNDS, NX, NY, 2, 8, 128), f32),
            pltpu.VMEM((ROUNDS, NY, NX, 2, 8, 128), f32),
            pltpu.VMEM((ROUNDS, 3, 4, 2, 8, 128), f32),
            pltpu.VMEM((ROUNDS, 3, 4, 2, 8, 128), f32),
            pltpu.VMEM((ROUNDS, 4, NX, 2, 8, 128), f32),
            pltpu.VMEM((ROUNDS, 4, NX, 2, 8, 128), f32),
            pltpu.VMEM((ROUNDS, NY, 2, 8, 128), f32),
            pltpu.VMEM((ROUNDS, NX, 2, 8, 128), f32),
            pltpu.VMEM((ROUNDS, 8, 256), bf16),
            pltpu.VMEM((ROUNDS, 8, 256), bf16),
            dma((NCHIP,)), dma((NCHIP,)), dma(()), dma(()), dma(()),
            dma((2, 2)), dma((2, 2)),
            dma((2, NSTEP)), dma((2, NSTEP + NPIECE)),
            dma((ROUNDS, 2, 3)), dma((ROUNDS, 2, 3)),
            dma((ROUNDS, 2, 4)), dma((ROUNDS, 2, 4)),
            dma((ROUNDS, NY)), dma((ROUNDS, NY)), dma((ROUNDS, NX)), dma((ROUNDS, NX)),
            dma((ROUNDS,)), dma((ROUNDS,)),
        ],
        compiler_params=pltpu.CompilerParams(collective_id=0, has_side_effects=True),
    )(tile_mask, tile_size, amplitudes, integrals)


def solution(mesh):
    axes = ("x", "zh", "zl", "y", "c")
    fine = Mesh(mesh.devices.reshape(NX, NZH, NZL, NY, NC), axes)
    return jax.shard_map(
        body,
        mesh=fine,
        in_specs=(P(axes, None), P(("zl", "y", "c"), ("x", "zh")), P(axes, None), P()),
        out_specs=P(axes, None),
        check_vma=False,
    )
```

time: 158 us -> 93.5 us (0.59)
  Pallas kernels: 156 us -> 91.9 us
    pallas_call x1, Pallas kernels: 156 us -> 91.9 us  [body(): pl.pallas_call(kernel, out_shape=jax.ShapeDtypeStruct((8, 2048), bf16), i...]
where the time goes in v2:
time: 93.5 us; the launch traced here: 93.3 us
  Pallas kernels  91.9 us (98%)
  local copies, waits for them, and re-layouts  1.38 us (1%)
    pallas_call x1, Pallas kernels, body(): pl.pallas_call(kernel, out_shape=jax.ShapeDtypeStruct((8, 2048), bf16), i...  91.9 us

profile of v2, /device:TPU:1, one launch (start us, length us, event | category | flops | bytes accessed | tf_op | source)
XLA Modules:
  0.0 93.3 jit_solution(1291990714910269280)
XLA Ops:
  0.0 91.9 %shard_map.46 = bf16[8,2048]{1,0:T(8,128)(2,1)} custom-call(s32[1,384]{1,0:T(1,128)} %mask_ref.1, s32[384]{0:T(512)} %size_ref.1, bf16[8,49152]{1,0:T(8,128)(2,1)} %amp_ref.1, bf16[768,128]{1,0:T(8,128)(2,1)} %int_ref.1), custom_call_target="tpu_custom_call" | custom-call | tf_op jit(solution)/shard_map/pallas_call | solution.py:365
  91.9 1.4 %copy.6 = bf16[8,2048]{1,0:T(8,128)(2,1)} copy(bf16[8,2048]{1,0:T(8,128)(2,1)} %shard_map.46) | data formatting | bytes 65536

commit v3 on v0

v3 whole, which is shorter than its diff:
```python
import jax
import jax.numpy as jnp
from jax import lax
from jax.experimental import pallas as pl
from jax.experimental.pallas import tpu as pltpu
from jax.sharding import Mesh, PartitionSpec as P

NX, NZH, NZL, NY, NC = 4, 4, 4, 8, 2
NZ = NZH * NZL
NCHIP = NX * NY
NPIECE = 4
FAR = NZ // 2
NSTEP = NPIECE * FAR
ROUNDS = NZH
MIXED = 2
MESH = pl.DeviceIdType.MESH


def kernel(mask_ref, size_ref, amp_ref, int_ref, out_ref,
           am, a2, bb, ca, rxp, rxm, fa, cb, ryp, rym, fb, sb, so,
           a_send, a_recv, a_loc, sib_send, sib_recv, b_send, b_recv,
           z_send, z_recv, x_send, x_recv, y_send, y_recv,
           ring_send, ring_recv, fb_send, fb_recv, o_send, o_recv, entered):
    x = lax.axis_index("x")
    zh = lax.axis_index("zh")
    zl = lax.axis_index("zl")
    y = lax.axis_index("y")
    c = lax.axis_index("c")
    z = zh * NZL + zl
    me = x * NY + y
    other = 1 - c

    barrier = pltpu.get_barrier_semaphore()

    for dy in range(1, NY):
        pl.semaphore_signal(barrier, inc=1, device_id={"y": lax.rem(y + dy, NY)}, device_id_type=MESH)
    for dx in range(NX):
        xx = lax.rem(x + dx, NX)
        if dx:
            pl.semaphore_signal(barrier, inc=1, device_id={"x": xx}, device_id_type=MESH)
        pl.semaphore_signal(barrier, inc=1, device_id={"x": xx, "c": other}, device_id_type=MESH)
    zup = lax.rem(z + 1, NZ)
    zdn = lax.rem(z + NZ - 1, NZ)
    up = {"zh": zup // NZL, "zl": lax.rem(zup, NZL)}
    dn = {"zh": zdn // NZL, "zl": lax.rem(zdn, NZL)}
    pl.semaphore_signal(barrier, inc=1, device_id=up, device_id_type=MESH)
    pl.semaphore_signal(barrier, inc=1, device_id=dn, device_id_type=MESH)

    pl.semaphore_wait(barrier, NY - 1 + 2 * NX - 1 + 2)
    for dx in range(1, NX):
        pl.semaphore_signal(entered, inc=1, device_id={"x": lax.rem(x + dx, NX)}, device_id_type=MESH)

    jb = lax.rem(x, 2)
    cdst = x // 2

    def b_src(h, part):
        return int_ref.at[(2 * h + part) * 192:(2 * h + part + 1) * 192, :]

    def b_copy(h, part):
        return pltpu.make_async_remote_copy(
            src_ref=b_src(h, part), dst_ref=bb.at[jb, z, part],
            send_sem=b_send.at[h, part], recv_sem=b_recv.at[jb, part],
            device_id={"x": 2 * c + h, "c": cdst}, device_id_type=MESH)

    def b_stays(h):
        return x == 2 * c + h

    for h in range(2):
        @pl.when(b_stays(h))
        def _():
            for part in range(2):
                pltpu.make_async_copy(b_src(h, part), bb.at[jb, z, part], b_recv.at[jb, part]).start()

    for part in range(2):
        for h in range(2):
            @pl.when(jnp.logical_not(b_stays(h)))
            def _():
                b_copy(h, part).start()

    lane = lax.broadcasted_iota(jnp.int32, (8, 128), 1)

    def live(q, _):
        for t in range(12):
            tile = ((t // 3) * 2 * NY + 2 * lax.rem(q, NY)) * 6 + (q // NY) * 3 + t % 3
            limit = jnp.where(mask_ref[0, tile] == 1, size_ref[tile], 0)
            col = pl.multiple_of(tile * 128, 128)
            v = amp_ref[:, pl.ds(col, 128)].astype(jnp.float32)
            am[q, :, t * 128:(t + 1) * 128] = jnp.where(lane < limit, v, 0.0).astype(jnp.bfloat16)
        return 0

    lax.fori_loop(0, NCHIP, live, 0)
    def a_copy(i):
        xx = lax.rem(x + i // NY, NX)
        yy = lax.rem(y + lax.rem(i, NY), NY)
        return pltpu.make_async_remote_copy(
            src_ref=am.at[xx * NY + yy], dst_ref=a2.at[c, pl.ds(pl.multiple_of(me * 8, 8), 8), :],
            send_sem=a_send.at[i], recv_sem=a_recv.at[i],
            device_id={"x": xx, "y": yy}, device_id_type=MESH)

    def a_start(i, _):
        a_copy(i).start()
        return 0

    pl.semaphore_wait(entered, NX - 1)
    lax.fori_loop(1, NCHIP, a_start, 0)
    a_own = pltpu.make_async_copy(am.at[me], a2.at[c, pl.ds(pl.multiple_of(me * 8, 8), 8), :], a_loc)
    a_own.start()

    sib_copy = pltpu.make_async_remote_copy(
        src_ref=a2.at[c], dst_ref=a2.at[c], send_sem=sib_send, recv_sem=sib_recv,
        device_id={"c": other}, device_id_type=MESH)

    def a_finish():
        def a_wait(i, _):
            a_copy(i).wait_recv()
            return 0
        lax.fori_loop(1, NCHIP, a_wait, 0)
        a_own.wait()
        sib_copy.start()

    behind = [[z] + [lax.rem(z + (NZ - d if way == 0 else d), NZ) for d in range(1, FAR + 1)] for way in range(2)]

    def z_ref(n, way):
        i = n % NPIECE
        return bb.at[i % 2, behind[way][n // NPIECE], i // 2]

    def z_copy(n, way):
        ref = z_ref(n, way)
        return pltpu.make_async_remote_copy(
            src_ref=ref, dst_ref=ref, send_sem=z_send.at[way, n], recv_sem=z_recv.at[way, n + NPIECE],
            device_id=up if way == 0 else dn, device_id_type=MESH)

    def z_arrive(n, way):
        ref = z_ref(n, way)
        pltpu.make_async_copy(ref, ref, z_recv.at[way, n]).wait()

    def z_passes(n, way):
        near = (n % NPIECE < NPIECE // 2) == (way == 0)
        return n < NSTEP - NPIECE or near

    def z_slots(lo, hi):
        for n in range(lo * NPIECE // 4, hi * NPIECE // 4):
            if n < NPIECE:
                ref = z_ref(n, 0)
                pltpu.make_async_copy(ref, ref, b_recv.at[n % 2, n // 2]).wait()
            for way in range(2):
                if n >= NPIECE:
                    z_arrive(n, way)
                if z_passes(n, way):
                    z_copy(n, way).start()

    def z_far():
        for i in range(NPIECE):
            z_arrive(NSTEP + i, 0 if i < NPIECE // 2 else 1)

    side = jnp.where(zl < NZL // 2, NZH - 1, 1)
    block = [zh, lax.rem(zh + side, NZH), lax.rem(zh + NZH - side, NZH), lax.rem(zh + NZH // 2, NZH)]

    xs = [lax.rem(x + d, NX) for d in range(NX)]
    ys = [lax.rem(y + d, NY) for d in range(NY)]

    def x_copy(r, h, way, m):
        if way == 0:
            src = (ca.at[r, h, xs[2], 0:4], ca.at[r, h, xs[1], 4:8], ca.at[r, h, xs[1], 0:4])[m]
        else:
            src = (ca.at[r, h, xs[2], 4:8], ca.at[r, h, xs[3], 0:4], ca.at[r, h, xs[3], 4:8])[m]
        return pltpu.make_async_remote_copy(
            src_ref=src, dst_ref=(rxp, rxm)[way].at[r, h, m],
            send_sem=x_send.at[r, h, way, m], recv_sem=x_recv.at[r, h, way, m],
            device_id={"x": xs[1] if way == 0 else xs[3]}, device_id_type=MESH)

    def y_copy(r, h, d):
        return pltpu.make_async_remote_copy(
            src_ref=ca.at[r, h, x, ys[d]], dst_ref=fa.at[r, h, d],
            send_sem=y_send.at[r, h, d], recv_sem=y_recv.at[r, h, d],
            device_id={"y": ys[d]}, device_id_type=MESH)

    def ring_copy(way, m):
        row = ys[4 - m] if way == 0 else ys[4 + m]
        buf = (ryp, rym)[way]
        part = slice(2 * way, 2 * way + 2) if m == 0 else slice(0, NX)
        return pltpu.make_async_remote_copy(
            src_ref=cb.at[row, part], dst_ref=buf.at[m, part],
            send_sem=ring_send.at[way, m], recv_sem=ring_recv.at[way, m],
            device_id={"y": ys[1] if way == 0 else ys[7]}, device_id_type=MESH)

    def fb_copy(d):
        return pltpu.make_async_remote_copy(
            src_ref=cb.at[y, xs[d]], dst_ref=fb.at[d], send_sem=fb_send.at[d], recv_sem=fb_recv.at[d],
            device_id={"x": xs[d]}, device_id_type=MESH)

    def ring_next(m):
        for way in range(2):
            row = ys[4 - m] if way == 0 else ys[4 + m]
            buf = (ryp, rym)[way]
            ring_copy(way, m - 1).wait_recv()
            part = slice(2 * way, 2 * way + 2) if m == 1 else slice(0, NX)
            cb[row, part] = cb[row, part] + buf[m - 1, part]
            ring_copy(way, m).start()

    def ring_last():
        ring_copy(0, 3).wait_recv()
        ring_copy(1, 3).wait_recv()
        cb[y] = cb[y] + ryp[3] + rym[3]
        for d in (2, 1, 3):
            fb_copy(d).start()

    def halves(r):
        return (0,) if r == MIXED else (0, 1)

    def o_copy(r):
        return pltpu.make_async_remote_copy(
            src_ref=sb.at[r], dst_ref=so.at[r], send_sem=o_send.at[r], recv_sem=o_recv.at[r],
            device_id={"c": other}, device_id_type=MESH)

    def first(r):
        rhs = jnp.concatenate([bb[0, pl.ds(NZL * block[r], NZL)].reshape(1536, 128), bb[1, pl.ds(NZL * block[r], NZL)].reshape(1536, 128)], axis=1)
        for cc in range(2):
            part = jnp.dot(a2[cc], rhs, preferred_element_type=jnp.float32).reshape(NX, NY, 8, 256)
            for h in halves(r):
                ca[r, h, :, :, cc] = part[:, :, :, h * 128:(h + 1) * 128]
            if r == MIXED:
                for xx in range(NX):
                    cb[:, xx, cc] = part[xx, :, :, 128:]
        if r == MIXED:
            ring_copy(0, 0).start()
            ring_copy(1, 0).start()
        for h in halves(r):
            for m in range(2):
                x_copy(r, h, 0, m).start()
                x_copy(r, h, 1, m).start()

    def second(r):
        for h in halves(r):
            x_copy(r, h, 0, 0).wait_recv()
            ca[r, h, xs[1], 0:4] = ca[r, h, xs[1], 0:4] + rxp[r, h, 0]
            x_copy(r, h, 0, 2).start()
            x_copy(r, h, 1, 0).wait_recv()
            ca[r, h, xs[3], 4:8] = ca[r, h, xs[3], 4:8] + rxm[r, h, 0]
            x_copy(r, h, 1, 2).start()

    def third(r):
        for h in halves(r):
            for m in range(1, 3):
                x_copy(r, h, 0, m).wait_recv()
                x_copy(r, h, 1, m).wait_recv()
            ca[r, h, x, 0:4] = ca[r, h, x, 0:4] + rxp[r, h, 2] + rxm[r, h, 1]
            ca[r, h, x, 4:8] = ca[r, h, x, 4:8] + rxp[r, h, 1] + rxm[r, h, 2]
            for d in (4, 3, 5, 2, 6, 1, 7):
                y_copy(r, h, d).start()

    def store(r, core, h, value):
        col = ((2 * core + h) * NZH + block[r]) * 128
        out_ref[:, pl.ds(pl.multiple_of(col, 128), 128)] = value

    def finish(r):
        for h in halves(r):
            for d in range(1, NY):
                y_copy(r, h, d).wait_recv()
        if r == MIXED:
            for d in range(1, NX):
                fb_copy(d).wait_recv()

        def rows(h, core):
            if h not in halves(r):
                total = cb[y, x, core]
                for d in range(1, NX):
                    total = total + fb[d, core]
                return total.astype(jnp.bfloat16)
            total = ca[r, h, x, y, core]
            for d in range(1, NY):
                total = total + fa[r, h, d, core]
            return total.astype(jnp.bfloat16)

        for h in range(2):
            sb[r, :, h * 128:(h + 1) * 128] = rows(h, other)
        o_copy(r).start()
        for h in range(2):
            store(r, c, h, rows(h, c))

    z_slots(0, 25)
    a_finish()
    z_slots(25, 26)
    sib_copy.wait_recv()
    first(0)
    z_slots(26, 28)
    first(1)
    z_slots(28, 30)
    second(0)
    z_slots(30, 32)
    first(2)
    second(1)
    third(0)
    z_far()
    first(3)
    ring_next(1)
    third(1)
    second(2)
    ring_next(2)
    second(3)
    finish(0)
    third(2)
    ring_next(3)
    finish(1)
    third(3)
    ring_last()
    finish(2)
    finish(3)

    for r in range(ROUNDS):
        o_copy(r).wait_recv()
        for h in range(2):
            store(r, other, h, so[r, :, h * 128:(h + 1) * 128])

    def a_left(i, _):
        a_copy(i).wait_send()
        return 0

    lax.fori_loop(1, NCHIP, a_left, 0)
    sib_copy.wait_send()

    for h in range(2):
        @pl.when(jnp.logical_not(b_stays(h)))
        def _():
            for part in range(2):
                b_copy(h, part).wait_send()

    for n in range(NSTEP):
        for way in range(2):
            if z_passes(n, way):
                z_copy(n, way).wait_send()
    for r in range(ROUNDS):
        for h in halves(r):
            for way in range(2):
                for m in range(3):
                    x_copy(r, h, way, m).wait_send()
            for d in range(1, NY):
                y_copy(r, h, d).wait_send()
        o_copy(r).wait_send()
    for way in range(2):
        for m in range(4):
            ring_copy(way, m).wait_send()
    for d in range(1, NX):
        fb_copy(d).wait_send()


def body(amplitudes, integrals, tile_mask, tile_size):
    dma = pltpu.SemaphoreType.DMA
    f32, bf16 = jnp.float32, jnp.bfloat16
    return pl.pallas_call(
        kernel,
        out_shape=jax.ShapeDtypeStruct((8, 2048), bf16),
        in_specs=[pl.BlockSpec(memory_space=pltpu.SMEM)] * 2 + [pl.BlockSpec(memory_space=pltpu.VMEM)] * 2,
        out_specs=pl.BlockSpec(memory_space=pltpu.VMEM),
        scratch_shapes=[
            pltpu.VMEM((NCHIP, 8, 1536), bf16),
            pltpu.VMEM((2, 256, 1536), bf16),
            pltpu.VMEM((2, NZ, 2, 192, 128), bf16),
            pltpu.VMEM((ROUNDS, 2, NX, NY, 2, 8, 128), f32),
            pltpu.VMEM((ROUNDS, 2, 3, 4, 2, 8, 128), f32),
            pltpu.VMEM((ROUNDS, 2, 3, 4, 2, 8, 128), f32),
            pltpu.VMEM((ROUNDS, 2, NY, 2, 8, 128), f32),
            pltpu.VMEM((NY, NX, 2, 8, 128), f32),
            pltpu.VMEM((4, NX, 2, 8, 128), f32),
            pltpu.VMEM((4, NX, 2, 8, 128), f32),
            pltpu.VMEM((NX, 2, 8, 128), f32),
            pltpu.VMEM((ROUNDS, 8, 256), bf16),
            pltpu.VMEM((ROUNDS, 8, 256), bf16),
            dma((NCHIP,)), dma((NCHIP,)), dma(()), dma(()), dma(()),
            dma((2, 2)), dma((2, 2)),
            dma((2, NSTEP)), dma((2, NSTEP + NPIECE)),
            dma((ROUNDS, 2, 2, 3)), dma((ROUNDS, 2, 2, 3)),
            dma((ROUNDS, 2, NY)), dma((ROUNDS, 2, NY)),
            dma((2, 4)), dma((2, 4)), dma((NX,)), dma((NX,)),
            dma((ROUNDS,)), dma((ROUNDS,)), pltpu.SemaphoreType.REGULAR,
        ],
        compiler_params=pltpu.CompilerParams(collective_id=0, has_side_effects=True),
    )(tile_mask, tile_size, amplitudes, integrals)


def solution(mesh):
    axes = ("x", "zh", "zl", "y", "c")
    fine = Mesh(mesh.devices.reshape(NX, NZH, NZL, NY, NC), axes)
    return jax.shard_map(
        body,
        mesh=fine,
        in_specs=(P(axes, None), P(("zl", "y", "c"), ("x", "zh")), P(axes, None), P()),
        out_specs=P(axes, None),
        check_vma=False,
    )
```

time: 456 us -> 88 us (0.19)
  waiting for transfers between devices: 384 us -> 0 us
  Pallas kernels: 0 us -> 86.4 us
  blocking collectives: 44.1 us -> 0 us
  between operations: 13.4 us -> 0.01 us
  matrix products: 5.62 us -> 0 us
    reduce_scatter x1 -> x0, waiting for transfers between devices: 292 us -> none  [body(): lax.psum_scatter(partial_value, 'grp', scatter_dimension=0, tiled=True)]
    all_gather x1 -> x0, waiting for transfers between devices: 90.9 us -> none  [body(): lax.all_gather(integrals, 'blk', axis=1, tiled=True)]
    pallas_call x0 -> x1, Pallas kernels: none -> 86.4 us  [body(): pl.pallas_call(kernel, out_shape=jax.ShapeDtypeStruct((8, 2048), bf16), i...]
    all_to_all x1 -> x0, blocking collectives: 44.1 us -> none  [body(): lax.all_to_all(masked, 'grp', split_axis=1, concat_axis=0, tiled=True)]
    dot_general x1 -> x0, matrix products: 5.62 us -> none  [body(): jnp.dot(regrouped, lax.all_gather(integrals, 'blk', axis=1, tiled=True),...]
  transfers between devices with their start and end apart: 2 -> 0, of which waited for: 2 -> 0; matrix products, arithmetic and copies ran while one was open for 1% -> 0% of each run, Pallas kernels for 0% -> 0%
where the time goes in v3:
time: 88 us; the launch traced here: 87.8 us
  Pallas kernels  86.4 us (98%)
  local copies, waits for them, and re-layouts  1.38 us (2%)
    pallas_call x1, Pallas kernels, body(): pl.pallas_call(kernel, out_shape=jax.ShapeDtypeStruct((8, 2048), bf16), i...  86.4 us

profile of v3, /device:TPU:1, one launch (start us, length us, event | category | flops | bytes accessed | tf_op | source)
XLA Modules:
  0.0 87.8 jit_solution(6833348438512264317)
XLA Ops:
  0.0 86.4 %shard_map.46 = bf16[8,2048]{1,0:T(8,128)(2,1)} custom-call(s32[1,384]{1,0:T(1,128)} %mask_ref.1, s32[384]{0:T(512)} %size_ref.1, bf16[8,49152]{1,0:T(8,128)(2,1)} %amp_ref.1, bf16[768,128]{1,0:T(8,128)(2,1)} %int_ref.1), custom_call_target="tpu_custom_call" | custom-call | tf_op jit(solution)/shard_map/pallas_call | solution.py:350
  86.4 1.4 %copy.6 = bf16[8,2048]{1,0:T(8,128)(2,1)} copy(bf16[8,2048]{1,0:T(8,128)(2,1)} %shard_map.46) | data formatting | bytes 65536

commit v4 on v3

--- a/solution.py
+++ b/solution.py
@@ -20,7 +20,7 @@
            am, a2, bb, ca, rxp, rxm, fa, cb, ryp, rym, fb, sb, so,
            a_send, a_recv, a_loc, sib_send, sib_recv, b_send, b_recv,
            z_send, z_recv, x_send, x_recv, y_send, y_recv,
-           ring_send, ring_recv, fb_send, fb_recv, o_send, o_recv, entered):
+           ring_send, ring_recv, fb_send, fb_recv, o_send, o_recv, near, far, entered):
     x = lax.axis_index("x")
     zh = lax.axis_index("zh")
     zl = lax.axis_index("zl")
@@ -32,7 +32,7 @@
 
     barrier = pltpu.get_barrier_semaphore()
 
-    for dy in range(1, NY):
+    for dy in (1, NY - 1):
         pl.semaphore_signal(barrier, inc=1, device_id={"y": lax.rem(y + dy, NY)}, device_id_type=MESH)
     for dx in range(NX):
         xx = lax.rem(x + dx, NX)
@@ -46,9 +46,9 @@
     pl.semaphore_signal(barrier, inc=1, device_id=up, device_id_type=MESH)
     pl.semaphore_signal(barrier, inc=1, device_id=dn, device_id_type=MESH)
 
-    pl.semaphore_wait(barrier, NY - 1 + 2 * NX - 1 + 2)
-    for dx in range(1, NX):
-        pl.semaphore_signal(entered, inc=1, device_id={"x": lax.rem(x + dx, NX)}, device_id_type=MESH)
+    pl.semaphore_wait(barrier, 2 + 2 * NX - 1 + 2)
+    for dy in (1, NY - 1):
+        pl.semaphore_signal(near, inc=1, device_id={"y": lax.rem(y + dy, NY)}, device_id_type=MESH)
 
     jb = lax.rem(x, 2)
     cdst = x // 2
@@ -101,6 +101,12 @@
         a_copy(i).start()
         return 0
 
+    pl.semaphore_wait(near, 2)
+    for dy in (2, NY - 2):
+        pl.semaphore_signal(far, inc=1, device_id={"y": lax.rem(y + dy, NY)}, device_id_type=MESH)
+    pl.semaphore_wait(far, 2)
+    for dx in range(1, NX):
+        pl.semaphore_signal(entered, inc=1, device_id={"x": lax.rem(x + dx, NX)}, device_id_type=MESH)
     pl.semaphore_wait(entered, NX - 1)
     lax.fori_loop(1, NCHIP, a_start, 0)
     a_own = pltpu.make_async_copy(am.at[me], a2.at[c, pl.ds(pl.multiple_of(me * 8, 8), 8), :], a_loc)
@@ -373,6 +379,7 @@
             dma((ROUNDS, 2, NY)), dma((ROUNDS, 2, NY)),
             dma((2, 4)), dma((2, 4)), dma((NX,)), dma((NX,)),
             dma((ROUNDS,)), dma((ROUNDS,)), pltpu.SemaphoreType.REGULAR,
+            pltpu.SemaphoreType.REGULAR, pltpu.SemaphoreType.REGULAR,
         ],
         compiler_params=pltpu.CompilerParams(collective_id=0, has_side_effects=True),
     )(tile_mask, tile_size, amplitudes, integrals)

time: 88 us -> 89.8 us (1.020)
  Pallas kernels: 86.4 us -> 88.2 us
    pallas_call x1, Pallas kernels: 86.4 us -> 88.2 us  [body(): pl.pallas_call(kernel, out_shape=jax.ShapeDtypeStruct((8, 2048), bf16), i...]
where the time goes in v4:
time: 89.8 us; the launch traced here: 89.6 us
  Pallas kernels  88.2 us (98%)
  local copies, waits for them, and re-layouts  1.38 us (2%)
    pallas_call x1, Pallas kernels, body(): pl.pallas_call(kernel, out_shape=jax.ShapeDtypeStruct((8, 2048), bf16), i...  88.2 us

profile of v4, /device:TPU:1, one launch (start us, length us, event | category | flops | bytes accessed | tf_op | source)
XLA Modules:
  0.0 89.6 jit_solution(6258703438798395490)
XLA Ops:
  0.0 88.2 %shard_map.46 = bf16[8,2048]{1,0:T(8,128)(2,1)} custom-call(s32[1,384]{1,0:T(1,128)} %mask_ref.1, s32[384]{0:T(512)} %size_ref.1, bf16[8,49152]{1,0:T(8,128)(2,1)} %amp_ref.1, bf16[768,128]{1,0:T(8,128)(2,1)} %int_ref.1), custom_call_target="tpu_custom_call" | custom-call | tf_op jit(solution)/shard_map/pallas_call | solution.py:356
  88.2 1.4 %copy.6 = bf16[8,2048]{1,0:T(8,128)(2,1)} copy(bf16[8,2048]{1,0:T(8,128)(2,1)} %shard_map.46) | data formatting | bytes 65536
